TPU v7x, 32 devices: a whole 2x2x4 slice. The times are simulated.
32 devices in a mesh: tm: 4 (over y, x), pair: 8 (over z, core).
Axes of the slice: x: 2, y: 2, z: 4, core: 2. Of those that a mesh axis runs over, the one named last changes fastest.
Arguments:
- three_center: bfloat16 [192, 64, 1024], P('pair'), may hold values from -6 to 6
- green_occ: bfloat16 [4, 64, 64, 64], P('tm'), may hold values from -0.75 to 0.75
- green_vir: bfloat16 [4, 64, 64, 64], P('tm'), may hold values from -0.75 to 0.75
- pair_list: int32 [192], P('pair'), may hold values from 0 to 63
- block_counts: int32 [8], P('pair'), may hold values from 6 to 24, as said below
- cosine_weights: float32 [4, 4], replicated, may hold values from -3 to 3
- coulomb_rows: int32 [8, 3], replicated, may hold values from 0 to 7, as said below
- coulomb_blocks: float32 [8, 3, 128, 128], replicated, may hold values from -0.3125 to 0.3125
Outputs:
- screened: float32 [4, 1024, 1024], P('tm', 'pair')
Inputs may be any that keep to these rules, and one draw needn't show every extreme that they name: `block_counts`: slots from the count on are not used; some index of pair has all 24 slots live. `coulomb_rows`: the row blocks of one column block are distinct, and the first is the column block itself.
All inputs are finite; a program needn't handle non-finite values.
Results may differ from a plain program's by a relative error of at most 0.0041.
Values sent between devices are 32-bit elements; how exact they have to be, the bound alone decides.
A program may use at most 64 MiB of HBM per device.

v0:
```python
import math

import jax
import jax.numpy as jnp
from jax import lax
from jax.sharding import PartitionSpec as P


def half_product(green_matrix, pair_list, alive_mask, three_center):
    picked = green_matrix[0][pair_list]
    product = jnp.einsum("bij,bjp->bip", picked, three_center, preferred_element_type=jnp.float32)
    product = product * alive_mask[:, None, None]
    return product.astype(jnp.bfloat16).reshape(-1, three_center.shape[2])


def local(
    three_center,
    green_occ,
    green_vir,
    pair_list,
    block_counts,
    cosine_weights,
    coulomb_rows,
    coulomb_blocks,
):
    slots = three_center.shape[0]
    pair_devices = lax.axis_size("pair")
    alive_mask = (jnp.arange(slots, dtype=jnp.int32) < block_counts[0]).astype(jnp.float32)
    left_side = half_product(green_occ, pair_list, alive_mask, three_center)
    right_side = half_product(green_vir, pair_list, alive_mask, three_center)
    normalizer = 1.0 / math.sqrt(slots * three_center.shape[1] * pair_devices)
    summed = lax.dot_general(
        left_side, right_side, (((0,), (0,)), ((), ())), preferred_element_type=jnp.float32
    )
    row_slab = lax.psum_scatter(summed * normalizer, "pair", scatter_dimension=0, tiled=True)
    transformed = jnp.einsum(
        "ft,trc->frc",
        cosine_weights,
        lax.all_to_all(row_slab[None], "tm", split_axis=2, concat_axis=0, tiled=True),
        precision=lax.Precision.HIGHEST,
    )
    spectra = lax.all_to_all(transformed, "tm", split_axis=0, concat_axis=2, tiled=True)
    rows_here = spectra.shape[1]
    column_blocks = coulomb_rows.shape[0]
    per_column = coulomb_rows.shape[1]
    block_width = coulomb_blocks.shape[2]
    blocked = spectra.reshape(rows_here, column_blocks, block_width)
    gathered = jnp.take(blocked, coulomb_rows.reshape(-1), axis=1)
    factors = coulomb_blocks.reshape(column_blocks * per_column, block_width, block_width)
    screened = jnp.einsum("mjx,jxy->mjy", gathered, factors, precision=lax.Precision.HIGHEST)
    screened = screened.reshape(rows_here, column_blocks, per_column, block_width).sum(axis=2)
    return screened.reshape(1, rows_here, column_blocks * block_width)


def solution(mesh):
    return jax.shard_map(
        local,
        mesh=mesh,
        in_specs=(
            P("pair", None, None),
            P("tm", None, None, None),
            P("tm", None, None, None),
            P("pair"),
            P("pair"),
            P(),
            P(),
            P(),
        ),
        out_specs=P("tm", "pair", None),
        check_vma=False,
    )
```

profile of v0, /device:TPU:8, one launch (start us, length us, event | category | flops | bytes accessed | tf_op | source)
XLA Modules:
  0.0 126.6 jit_solution(750855462552319083)
XLA Ops:
  6.5 0.0 copy-start
  6.5 0.0 reduce-scatter.2.cloned.1.call-start
  6.5 0.8 compare_select_fusion.1
  7.4 2.0 %gather_fusion = bf16[24,64,64]{2,1,0:T(8,128)(2,1)S(1)} fusion(bf16[64,64,64]{2,1,0:T(8,128)(2,1)} %bitcast.43, s32[1024]{0:T(1024)S(1)} %pad_clamp_fusion.1), kind=kCustom, calls=%fused_computation | custom fusion | bytes 393312 | tf_op jit(solution)/shard_map/gather | solution.py:10
  9.3 2.6 %gather_fusion.1 = bf16[24,64,64]{2,1,0:T(8,128)(2,1)} fusion(bf16[64,64,64]{2,1,0:T(8,128)(2,1)} %bitcast.44, s32[1024]{0:T(1024)S(1)} %pad_clamp_fusion.1), kind=kCustom, calls=%fused_computation.1 | custom fusion | bytes 393312 | tf_op jit(solution)/shard_map/gather | solution.py:10
  12.6 0.0 copy-done
  12.6 8.2 %bitcast_multiply_fusion = f32[1024,1024]{1,0:T(8,128)} fusion(f32[24]{0:T(128)S(1)} %compare_convert_fusion, bf16[24,64,64]{2,1,0:T(8,128)(2,1)} %gather_fusion.1, bf16[24,64,1024]{2,1,0:T(8,128)(2,1)S(1)} %copy-done, bf16[24,64,64]{2,1,0:T(8,128)(2,1)S(1)} %gather_fusion), kind=kOutput, calls=%fused_computation.5 | convolution fusion | flops 3631218688 | bytes 7733344 | tf_op jit(solution)/shard_map/dot_general | solution.py:32
  20.8 0.0 copy-start.2
  20.8 0.0 copy-start.1
  20.8 0.0 reduce-scatter.2.cloned.1.call-update
  20.9 47.7 %reduce-scatter.2.cloned.1.call-done = f32[128,1024]{1,0:T(8,128)} async-done(((f32[1024,1024]{1,0:T(8,128)}), f32[128,1024]{1,0:T(8,128)}) %reduce-scatter.2.cloned.1.call-update) | async-done | bytes 524304 | tf_op jit(solution)/shard_map/reduce_scatter | solution.py:35
  68.6 1.9 %copy.20 = f32[1,128,1024]{1,0,2:T(1,128)} copy(f32[1,128,1024]{2,1,0:T(8,128)} %bitcast.42) | data formatting | bytes 1048576 | tf_op jit(solution)/shard_map/broadcast_in_dim | solution.py:39
  70.5 4.1 %all-to-all-start = ((f32[1,128,1024]{1,0,2:T(1,128)}), f32[1,128,1024]{1,0,2:T(1,128)}, u32[]{:S(2)}, u32[]{:S(2)}) async-start(f32[1,128,1024]{1,0,2:T(1,128)} %copy.20), calls=%async_computation.1 | async-start | bytes 1048576 | tf_op jit(solution)/shard_map/all_to_all | solution.py:39
  74.7 0.0 copy-done.2
  74.7 0.1 copy.19
  74.7 0.1 reshape.61
  74.8 8.2 %all-to-all-done = f32[1,128,1024]{1,0,2:T(1,128)} async-done(((f32[1,128,1024]{1,0,2:T(1,128)}), f32[1,128,1024]{1,0,2:T(1,128)}, u32[]{:S(2)}, u32[]{:S(2)}) %all-to-all-start) | async-done | bytes 524320 | tf_op jit(solution)/shard_map/all_to_all | solution.py:39
  83.1 2.0 %copy.28 = f32[1,128,4,256]{3,2,1,0:T(4,128)} copy(f32[1,128,4,256]{1,3,2,0:T(8,128)} %bitcast.5) | data formatting | bytes 1048576 | tf_op jit(solution)/shard_map/all_to_all | solution.py:39
  85.1 0.0 copy-done.1
  85.1 2.0 %convolution_bitcast_fusion = f32[4,128,256]{2,0,1:T(4,128)S(1)} fusion(f32[1,128,4,256]{3,2,1,0:T(4,128)} %copy.28, f32[4,4]{1,0:T(4,128)S(1)} %copy-done.1), kind=kOutput, calls=%fused_computation.13 | convolution fusion | flops 6291456 | bytes 1048640 | tf_op jit(solution)/shard_map/ft,trc->frc/dot_general | solution.py:36
  87.1 0.9 copy.22
  88.0 4.1 %all-to-all-start.1 = ((f32[4,128,256]{2,1,0:T(8,128)}), f32[4,128,256]{2,1,0:T(8,128)}, u32[]{:S(2)}, u32[]{:S(2)}) async-start(f32[4,128,256]{2,1,0:T(8,128)} %copy.22), calls=%async_computation.2 | async-start | bytes 1048576 | tf_op jit(solution)/shard_map/all_to_all | solution.py:42
  92.2 0.1 reshape.59
  92.3 9.3 %all-to-all-done.1 = f32[4,128,256]{2,1,0:T(8,128)} async-done(((f32[4,128,256]{2,1,0:T(8,128)}), f32[4,128,256]{2,1,0:T(8,128)}, u32[]{:S(2)}, u32[]{:S(2)}) %all-to-all-start.1) | async-done | bytes 524320 | tf_op jit(solution)/shard_map/all_to_all | solution.py:42
  101.6 2.0 %copy.23 = f32[4,128,256]{1,2,0:T(8,128)} copy(f32[4,128,256]{2,1,0:T(8,128)} %all-to-all-done.1) | data formatting | bytes 1048576 | tf_op jit(solution)/shard_map/all_to_all | solution.py:42
  103.7 2.0 %copy.25 = f32[128,8,128]{2,0,1:T(8,128)} copy(f32[128,8,128]{0,2,1:T(8,128)} %bitcast.39) | data formatting | bytes 1048576 | tf_op jit(solution)/shard_map/reshape | solution.py:47
  105.7 2.9 %gather_fusion.2 = f32[24,128,128]{2,1,0:T(8,128)} fusion(f32[128,8,128]{2,0,1:T(8,128)} %copy.25, s32[1024]{0:T(1024)S(1)} %pad_clamp_fusion), kind=kCustom, calls=%fused_computation.2 | custom fusion | bytes 3145824 | tf_op jit(solution)/shard_map/jit(_take)/gather | solution.py:48
  108.5 4.8 %fusion.6 = f32[24,128,128]{2,1,0:T(8,128)} fusion(f32[24,128,128]{2,1,0:T(8,128)} %bitcast.41, f32[24,128,128]{2,1,0:T(8,128)} %gather_fusion.2, pred[24]{0:T(512)(128)(4,1)S(1)} %compare_and_fusion), kind=kOutput, calls=%fused_computation.10 | convolution fusion | flops 604372992 | bytes 4718616 | tf_op jit(solution)/shard_map/mjx,jxy->mjy/dot_general | solution.py:50
  113.3 2.3 %reduce_sum.9 = f32[128,8,128]{2,0,1:T(8,128)} reduce(f32[128,8,3,128]{3,0,2,1:T(8,128)} %bitcast.38, f32[]{:T(128)} %constant.22.clone.1), dimensions={2}, to_apply=%region_1.2 | reduce | flops 262144 | bytes 2097156 | tf_op jit(solution)/shard_map/reduce_sum | solution.py:51
  115.6 2.0 %copy.26 = f32[128,8,128]{0,2,1:T(8,128)} copy(f32[128,8,128]{2,0,1:T(8,128)} %reduce_sum.9) | data formatting | bytes 1048576 | tf_op jit(solution)/shard_map/reduce_sum | solution.py:51
  117.7 2.0 %copy.27 = f32[1,128,1024]{2,1,0:T(8,128)} copy(f32[1,128,1024]{1,2,0:T(8,128)} %bitcast.40) | data formatting | bytes 1048576 | tf_op jit(solution)/shard_map/reshape | solution.py:52
  (5 shorter events, 0.0 us)
Async XLA Ops:
  6.5 6.1 %copy-start = (bf16[24,64,1024]{2,1,0:T(8,128)(2,1)S(1)}, bf16[24,64,1024]{2,1,0:T(8,128)(2,1)}, u32[]{:S(2)}) copy-start(bf16[24,64,1024]{2,1,0:T(8,128)(2,1)} %param.8) | copy-start | bytes 9437188
  6.5 62.0 %reduce-scatter.2.cloned.1.call-start = ((), (), s32[]{:S(2)}) async-start(), calls=%async_computation.3 | async-start | bytes 4718592 | tf_op jit(solution)/shard_map/reduce_scatter | solution.py:35
  20.8 53.8 %copy-start.2 = (s32[8,3]{0,1:T(4,128)S(1)}, s32[8,3]{0,1:T(4,128)}, u32[]{:S(2)}) copy-start(s32[8,3]{0,1:T(4,128)} %param.14) | copy-start | bytes 292
  20.8 64.2 %copy-start.1 = (f32[4,4]{1,0:T(4,128)S(1)}, f32[4,4]{1,0:T(4,128)}, u32[]{:S(2)}) copy-start(f32[4,4]{1,0:T(4,128)} %param.13) | copy-start | bytes 196
  70.5 12.5 %all-to-all-start = ((f32[1,128,1024]{1,0,2:T(1,128)}), f32[1,128,1024]{1,0,2:T(1,128)}, u32[]{:S(2)}, u32[]{:S(2)}) async-start(f32[1,128,1024]{1,0,2:T(1,128)} %copy.20), calls=%async_computation.1 | async-start | bytes 1048576 | tf_op jit(solution)/shard_map/all_to_all | solution.py:39
  88.0 13.6 %all-to-all-start.1 = ((f32[4,128,256]{2,1,0:T(8,128)}), f32[4,128,256]{2,1,0:T(8,128)}, u32[]{:S(2)}, u32[]{:S(2)}) async-start(f32[4,128,256]{2,1,0:T(8,128)} %copy.22), calls=%async_computation.2 | async-start | bytes 1048576 | tf_op jit(solution)/shard_map/all_to_all | solution.py:42
Sparse Core Ops, SparseCore 0:
  21.0 47.5 reduce-scatter.1
where the time goes:
time: 128 us; the launch traced here: 127 us
  waiting for transfers between devices  65.3 us (51%)
  local copies, waits for them, and re-layouts  20.7 us (16%)
  matrix products  15 us (12%)
  between operations  14.1 us (11%)
  starting transfers between devices  8.29 us (6%)
  other arithmetic  3.18 us (2%)
    reduce_scatter x1, waiting for transfers between devices, local(): lax.psum_scatter(summed * normalizer, 'pair', scatter_dimension=0, tiled=...  47.7 us
    all_to_all x1, waiting for transfers between devices, local(): lax.all_to_all(transformed, 'tm', split_axis=0, concat_axis=2, tiled=True)  9.32 us
    dot_general x1, matrix products, local(): lax.dot_general(left_side, right_side, (((0,), (0,)), ((), ())), preferre...  8.24 us
    all_to_all x1, waiting for transfers between devices, local(): lax.all_to_all(row_slab[None], 'tm', split_axis=2, concat_axis=0, tiled=T...  8.22 us
    dot_general x1, matrix products, local(): jnp.einsum('mjx,jxy->mjy', gathered, factors, precision=lax.Precision.HIG...  4.76 us
    gather x2, local copies, waits for them, and re-layouts, half_product(): picked = green_matrix[0][pair_list]  4.56 us
    all_to_all x1, starting transfers between devices, local(): lax.all_to_all(row_slab[None], 'tm', split_axis=2, concat_axis=0, tiled=T...  4.14 us
    all_to_all x1, starting transfers between devices, local(): lax.all_to_all(transformed, 'tm', split_axis=0, concat_axis=2, tiled=True)  4.14 us
  transfers between devices with their start and end apart: 3, of which 3 were waited for; matrix products, arithmetic and copies ran while one was open for 0% of the time, Pallas kernels for 0%

commit v1 on v0

--- a/solution.py
+++ b/solution.py
@@ -1,9 +1,14 @@
+import functools
 import math
 
 import jax
 import jax.numpy as jnp
 from jax import lax
+from jax.experimental import pallas as pl
+from jax.experimental.pallas import tpu as pltpu
 from jax.sharding import PartitionSpec as P
+
+MESH = pl.DeviceIdType.MESH
 
 
 def half_product(green_matrix, pair_list, alive_mask, three_center):
@@ -13,7 +18,7 @@
     return product.astype(jnp.bfloat16).reshape(-1, three_center.shape[2])
 
 
-def local(
+def collective_form(
     three_center,
     green_occ,
     green_vir,
@@ -52,7 +57,302 @@
     return screened.reshape(1, rows_here, column_blocks * block_width)
 
 
+def kernel(
+    times,
+    chips,
+    normalizer,
+    pair_list_ref,
+    counts_ref,
+    weights_ref,
+    factor_rows_ref,
+    three_ref,
+    occ_ref,
+    vir_ref,
+    coulomb_ref,
+    out_ref,
+    left,
+    right,
+    to_partner,
+    from_partner,
+    sums,
+    arrived,
+    peers_in,
+    spectra,
+    coulomb_high,
+    coulomb_low,
+    partner_send,
+    partner_recv,
+    chain_send,
+    chain_recv,
+    peer_send,
+    peer_recv,
+):
+    slots, width, panel = three_ref.shape
+    pieces, piece_rows = sums.shape[1], sums.shape[2]
+    rows = pieces * piece_rows
+    me = lax.axis_index("tm")
+    place = lax.axis_index("pair")
+    z = place // 2
+    core = place % 2
+    partner = z * 2 + 1 - core
+
+    barrier = pltpu.get_barrier_semaphore()
+    pl.semaphore_signal(barrier, inc=1, device_id={"pair": partner}, device_id_type=MESH)
+    for offset in range(1, times):
+        pl.semaphore_signal(
+            barrier, inc=1, device_id={"tm": (me + offset) % times}, device_id_type=MESH
+        )
+
+    @pl.when(z > 0)
+    def _():
+        pl.semaphore_signal(barrier, inc=1, device_id={"pair": place - 2}, device_id_type=MESH)
+
+    @pl.when(z < chips - 1)
+    def _():
+        pl.semaphore_signal(barrier, inc=1, device_id={"pair": place + 2}, device_id_type=MESH)
+
+    def half(slot, carry):
+        group = pair_list_ref[slot]
+        alive = (slot < counts_ref[0]).astype(jnp.float32)
+        both = jnp.concatenate([occ_ref[0, group], vir_ref[0, group]], axis=0)
+        product = jnp.dot(both, three_ref[slot], preferred_element_type=jnp.float32) * alive
+        product = product.astype(jnp.bfloat16)
+        here = pl.ds(pl.multiple_of(slot * width, width), width)
+        left[here, :] = product[:width]
+        right[here, :] = product[width:]
+        return carry
+
+    lax.fori_loop(0, slots, half, 0)
+
+    neighbours = (z > 0).astype(jnp.int32) + (z < chips - 1).astype(jnp.int32)
+    pl.semaphore_wait(barrier, times + neighbours)
+
+    def panel_slab(slab):
+        columns = pl.ds(pl.multiple_of(slab * rows, rows), rows)
+        product = lax.dot_general(
+            left[:, columns],
+            right[...],
+            (((0,), (0,)), ((), ())),
+            preferred_element_type=jnp.float32,
+        )
+        return (product * normalizer).reshape(pieces, piece_rows, panel)
+
+    def partner_copy(dest):
+        return pltpu.make_async_remote_copy(
+            src_ref=to_partner.at[dest],
+            dst_ref=from_partner.at[dest],
+            send_sem=partner_send.at[dest],
+            recv_sem=partner_recv.at[dest],
+            device_id={"pair": partner},
+            device_id_type=MESH,
+        )
+
+    def chain_copy(way, dest, piece):
+        return pltpu.make_async_remote_copy(
+            src_ref=sums.at[dest, piece],
+            dst_ref=arrived.at[way, dest, piece],
+            send_sem=chain_send.at[dest, piece],
+            recv_sem=chain_recv.at[way, dest, piece],
+            device_id={"pair": place + 2 - 4 * way},
+            device_id_type=MESH,
+        )
+
+    def peer_copy(offset, piece):
+        return pltpu.make_async_remote_copy(
+            src_ref=sums.at[z, piece],
+            dst_ref=peers_in.at[offset - 1, piece],
+            send_sem=peer_send.at[offset - 1, piece],
+            recv_sem=peer_recv.at[offset - 1, piece],
+            device_id={"tm": (me + offset) % times},
+            device_id_type=MESH,
+        )
+
+    low_half = (z < (chips + 1) // 2).astype(jnp.int32)
+
+    def slab_step(step, carry):
+        last = (step == chips - 1).astype(jnp.int32)
+        falling = chips - 1 - step
+        falling = falling - (falling <= z).astype(jnp.int32)
+        rising = step + (step >= z).astype(jnp.int32)
+        dest = last * z + (1 - last) * (low_half * falling + (1 - low_half) * rising)
+        to_partner[dest] = panel_slab(dest * 2 + 1 - core)
+        partner_copy(dest).start()
+        sums[dest] = panel_slab(dest * 2 + core)
+        partner_copy(dest).wait_recv()
+
+        def piece_step(piece, inner):
+            sums[dest, piece] = sums[dest, piece] + from_partner[dest, piece]
+
+            @pl.when(jnp.logical_and(z == 0, dest > 0))
+            def _():
+                chain_copy(0, dest, piece).start()
+
+            @pl.when(jnp.logical_and(z == chips - 1, dest < chips - 1))
+            def _():
+                chain_copy(1, dest, piece).start()
+
+            return inner
+
+        lax.fori_loop(0, pieces, piece_step, 0)
+        return carry
+
+    lax.fori_loop(0, chips, slab_step, 0)
+
+    blocks, per_block, cb = coulomb_ref.shape[0], coulomb_ref.shape[1], coulomb_ref.shape[2]
+    for block in range(blocks):
+        factor = coulomb_ref[block].reshape(per_block * cb, cb)
+        high = factor.astype(jnp.bfloat16)
+        coulomb_high[block] = high
+        coulomb_low[block] = (factor - high.astype(jnp.float32)).astype(jnp.bfloat16)
+
+    from_below = (z > 0).astype(jnp.int32) * (chips - 1 - z)
+    from_above = (z < chips - 1).astype(jnp.int32) * z
+    finish = jnp.maximum(from_below, from_above)
+
+    def chain_step(index, carry):
+        step = index // pieces
+        piece = index % pieces
+        for way in (0, 1):
+            dest = (chips - 1 - step) if way == 0 else step
+            if way == 0:
+                here = jnp.logical_and(z > 0, dest >= z)
+            else:
+                here = jnp.logical_and(z < chips - 1, dest <= z)
+
+            @pl.when(here)
+            def _():
+                chain_copy(way, dest, piece).wait_recv()
+                sums[dest, piece] = sums[dest, piece] + arrived[way, dest, piece]
+
+                @pl.when(dest != z)
+                def _():
+                    chain_copy(way, dest, piece).start()
+
+        @pl.when(step == finish)
+        def _():
+            for offset in range(1, times):
+                peer_copy(offset, piece).start()
+
+        return carry
+
+    lax.fori_loop(0, chips * pieces, chain_step, 0)
+
+    def mix_step(piece, carry):
+        mixed = sums[z, piece] * weights_ref[me, me]
+        for offset in range(1, times):
+            peer_copy(offset, piece).wait_recv()
+            mixed = mixed + peers_in[offset - 1, piece] * weights_ref[me, (me + times - offset) % times]
+        at = pl.ds(pl.multiple_of(piece * piece_rows, piece_rows), piece_rows)
+        for block in range(blocks):
+            spectra[block, at, :] = mixed[:, block * cb : (block + 1) * cb]
+        return carry
+
+    lax.fori_loop(0, pieces, mix_step, 0)
+
+    for block in range(blocks):
+        gathered = jnp.concatenate(
+            [spectra[factor_rows_ref[block, k]] for k in range(per_block)], axis=1
+        )
+        high = gathered.astype(jnp.bfloat16)
+        low = (gathered - high.astype(jnp.float32)).astype(jnp.bfloat16)
+        total = jnp.dot(high, coulomb_high[block], preferred_element_type=jnp.float32)
+        total += jnp.dot(low, coulomb_high[block], preferred_element_type=jnp.float32)
+        total += jnp.dot(high, coulomb_low[block], preferred_element_type=jnp.float32)
+        out_ref[0, :, block * cb : (block + 1) * cb] = total
+
+    def close_step(dest, carry):
+        partner_copy(dest).wait_send()
+
+        @pl.when(dest != z)
+        def _():
+            def close_piece(piece, inner):
+                chain_copy(0, dest, piece).wait_send()
+                return inner
+
+            lax.fori_loop(0, pieces, close_piece, 0)
+
+        return carry
+
+    lax.fori_loop(0, chips, close_step, 0)
+
+    def close_peers(piece, carry):
+        for offset in range(1, times):
+            peer_copy(offset, piece).wait_send()
+        return carry
+
+    lax.fori_loop(0, pieces, close_peers, 0)
+
+
+def kernel_form(
+    times,
+    pair_devices,
+    three_center,
+    green_occ,
+    green_vir,
+    pair_list,
+    block_counts,
+    cosine_weights,
+    coulomb_rows,
+    coulomb_blocks,
+):
+    slots, width, panel = three_center.shape
+    chips = pair_devices // 2
+    rows = panel // pair_devices
+    pieces = max(1, rows // 16)
+    piece_rows = rows // pieces
+    blocks, per_block, cb, _ = coulomb_blocks.shape
+    normalizer = 1.0 / math.sqrt(slots * width * pair_devices)
+    smem = pl.BlockSpec(memory_space=pltpu.SMEM)
+    vmem = pl.BlockSpec(memory_space=pltpu.VMEM)
+    slab = (pieces, piece_rows, panel)
+    return pl.pallas_call(
+        functools.partial(kernel, times, chips, normalizer),
+        out_shape=jax.ShapeDtypeStruct((1, rows, panel), jnp.float32),
+        in_specs=[smem] * 4 + [vmem] * 4,
+        out_specs=vmem,
+        scratch_shapes=[
+            pltpu.VMEM((slots * width, panel), jnp.bfloat16),
+            pltpu.VMEM((slots * width, panel), jnp.bfloat16),
+            pltpu.VMEM((chips,) + slab, jnp.float32),
+            pltpu.VMEM((chips,) + slab, jnp.float32),
+            pltpu.VMEM((chips,) + slab, jnp.float32),
+            pltpu.VMEM((2, chips) + slab, jnp.float32),
+            pltpu.VMEM((times - 1,) + slab, jnp.float32),
+            pltpu.VMEM((blocks, rows, cb), jnp.float32),
+            pltpu.VMEM((blocks, per_block * cb, cb), jnp.bfloat16),
+            pltpu.VMEM((blocks, per_block * cb, cb), jnp.bfloat16),
+            pltpu.SemaphoreType.DMA((chips,)),
+            pltpu.SemaphoreType.DMA((chips,)),
+            pltpu.SemaphoreType.DMA((chips, pieces)),
+            pltpu.SemaphoreType.DMA((2, chips, pieces)),
+            pltpu.SemaphoreType.DMA((times - 1, pieces)),
+            pltpu.SemaphoreType.DMA((times - 1, pieces)),
+        ],
+        compiler_params=pltpu.CompilerParams(
+            collective_id=0, has_side_effects=True, vmem_limit_bytes=60 * 1024 * 1024
+        ),
+    )(
+        pair_list,
+        block_counts,
+        cosine_weights,
+        coulomb_rows,
+        three_center,
+        green_occ,
+        green_vir,
+        coulomb_blocks,
+    )
+
+
 def solution(mesh):
+    times, pair_devices = mesh.shape["tm"], mesh.shape["pair"]
+
+    def local(*args):
+        rows = args[0].shape[2] // pair_devices
+        short = 4 <= pair_devices <= 16 and 2 <= times <= 4
+        if short and pair_devices % 2 == 0 and rows % 128 == 0:
+            return kernel_form(times, pair_devices, *args)
+        return collective_form(*args)
+
     return jax.shard_map(
         local,
         mesh=mesh,

time: 128 us -> 147 us (1.15)
  Pallas kernels: 0 us -> 143 us
  waiting for transfers between devices: 65.3 us -> 0 us
  local copies, waits for them, and re-layouts: 20.7 us -> 3.23 us
  matrix products: 15 us -> 0 us
  between operations: 14.1 us -> 0.66 us
  starting transfers between devices: 8.29 us -> 0 us
  other arithmetic: 3.18 us -> 0 us
    pallas_call x0 -> x1, Pallas kernels: none -> 143 us  [kernel_form(): pl.pallas_call(functools.partial(kernel, times, chips, normalizer), out_s...]
    reduce_scatter x1 -> x0, waiting for transfers between devices: 47.7 us -> none  [local(): lax.psum_scatter(summed * normalizer, 'pair', scatter_dimension=0, tiled=...]
    all_to_all x2 -> x0, waiting for transfers between devices: 17.5 us -> none  [the longest x1 9.32 us: local(): lax.all_to_all(transformed, 'tm', split_axis=0, concat_axis=2, tiled=True)]
    dot_general x3 -> x0, matrix products: 15 us -> none  [the longest x1 8.24 us: local(): lax.dot_general(left_side, right_side, (((0,), (0,)), ((), ())), preferre...]
    all_to_all x2 -> x0, starting transfers between devices: 8.29 us -> none  [the longest x1 4.14 us: local(): lax.all_to_all(row_slab[None], 'tm', split_axis=2, concat_axis=0, tiled=T...]
    gather x3 -> x0, local copies, waits for them, and re-layouts: 7.42 us -> none  [the longest x2 4.56 us: half_product(): picked = green_matrix[0][pair_list]]
    reshape x4 -> x0, local copies, waits for them, and re-layouts: 4.22 us -> none  [the longest x1 2.04 us: local(): return screened.reshape(1, rows_here, column_blocks * block_width)]
    all_to_all x2 -> x0, local copies, waits for them, and re-layouts: 4.07 us -> none  [the longest x1 2.04 us: local(): lax.all_to_all(row_slab[None], 'tm', split_axis=2, concat_axis=0, tiled=T...]
  transfers between devices with their start and end apart: 3 -> 0, of which waited for: 3 -> 0; matrix products, arithmetic and copies ran while one was open for 0% -> 0% of each run, Pallas kernels for 0% -> 0%
where the time goes in v1:
time: 147 us
  Pallas kernels  143 us (97%)
  local copies, waits for them, and re-layouts  3.23 us (2%)
    pallas_call x1, Pallas kernels, kernel_form(): pl.pallas_call(functools.partial(kernel, times, chips, normalizer), out_s...  143 us
    unnamed x2, local copies, waits for them, and re-layouts  3.23 us

profile of v1, /device:TPU:8, one launch (start us, length us, event | category | flops | bytes accessed | tf_op | source)
XLA Modules:
  0.0 146.5 jit_solution(1074465691914462572)
XLA Ops:
  0.7 1.3 copy.9.factor_rows_ref
  2.0 142.6 %shard_map.82 = f32[1,128,1024]{2,1,0:T(8,128)} custom-call(s32[24]{0:T(128)} %pair_list_ref.1, s32[1]{0:T(128)S(6)} %copy.11.counts_ref, f32[4,4]{1,0:T(4,128)} %weights_ref.1, s32[8,3]{1,0:T(8,128)} %copy.9.factor_rows_ref, bf16[24,64,1024]{2,1,0:T(8,128)(2,1)} %three_ref.1, bf16[1,64,64,64]{3,2,1,0:T(8,128)(2,1)} %occ_ref.1, ...), custom_call_target="tpu_custom_call" | custom-call | tf_op jit(solution)/shard_map/pallas_call | solution.py:308
  144.7 1.9 %copy.12 = f32[1,128,1024]{2,1,0:T(8,128)} copy(f32[1,128,1024]{2,1,0:T(8,128)} %shard_map.82) | data formatting | bytes 1048576

commit v2 on v1

--- a/solution.py
+++ b/solution.py
@@ -9,6 +9,25 @@
 from jax.sharding import PartitionSpec as P
 
 MESH = pl.DeviceIdType.MESH
+SPREAD = 3
+LAG = 2
+
+
+def slab_order(chips):
+    order, slots = [], []
+    for z in range(chips):
+        need = []
+        for dest in range(chips):
+            at = []
+            if dest > z or (dest == z and z > 0):
+                at.append(SPREAD * (chips - 1 - dest) + LAG * max(z - 1, 0))
+            if dest < z or (dest == z and z < chips - 1):
+                at.append(SPREAD * dest + LAG * max(chips - 2 - z, 0))
+            need.append((min(at), dest))
+        need.sort()
+        order.append([dest for _, dest in need])
+        slots.append([at for at, _ in need])
+    return order, [min(column) for column in zip(*slots)]
 
 
 def half_product(green_matrix, pair_list, alive_mask, three_center):
@@ -167,75 +186,82 @@
             device_id_type=MESH,
         )
 
-    low_half = (z < (chips + 1) // 2).astype(jnp.int32)
+    blocks, per_block, cb = coulomb_ref.shape[0], coulomb_ref.shape[1], coulomb_ref.shape[2]
+
+    def split_factor():
+        for block in range(blocks):
+            factor = coulomb_ref[block].reshape(per_block * cb, cb)
+            high = factor.astype(jnp.bfloat16)
+            coulomb_high[block] = high
+            coulomb_low[block] = (factor - high.astype(jnp.float32)).astype(jnp.bfloat16)
+
+    order, ready = slab_order(chips)
 
     def slab_step(step, carry):
-        last = (step == chips - 1).astype(jnp.int32)
-        falling = chips - 1 - step
-        falling = falling - (falling <= z).astype(jnp.int32)
-        rising = step + (step >= z).astype(jnp.int32)
-        dest = last * z + (1 - last) * (low_half * falling + (1 - low_half) * rising)
+        dest = 0
+        for row in range(chips):
+            for k in range(chips):
+                hit = jnp.logical_and(z == row, step == k).astype(jnp.int32)
+                dest = dest + order[row][k] * hit
         to_partner[dest] = panel_slab(dest * 2 + 1 - core)
         partner_copy(dest).start()
         sums[dest] = panel_slab(dest * 2 + core)
         partner_copy(dest).wait_recv()
-
-        def piece_step(piece, inner):
-            sums[dest, piece] = sums[dest, piece] + from_partner[dest, piece]
-
-            @pl.when(jnp.logical_and(z == 0, dest > 0))
-            def _():
-                chain_copy(0, dest, piece).start()
-
-            @pl.when(jnp.logical_and(z == chips - 1, dest < chips - 1))
-            def _():
-                chain_copy(1, dest, piece).start()
-
-            return inner
-
-        lax.fori_loop(0, pieces, piece_step, 0)
-        return carry
-
-    lax.fori_loop(0, chips, slab_step, 0)
-
-    blocks, per_block, cb = coulomb_ref.shape[0], coulomb_ref.shape[1], coulomb_ref.shape[2]
-    for block in range(blocks):
-        factor = coulomb_ref[block].reshape(per_block * cb, cb)
-        high = factor.astype(jnp.bfloat16)
-        coulomb_high[block] = high
-        coulomb_low[block] = (factor - high.astype(jnp.float32)).astype(jnp.bfloat16)
-
-    from_below = (z > 0).astype(jnp.int32) * (chips - 1 - z)
-    from_above = (z < chips - 1).astype(jnp.int32) * z
+        sums[dest] = sums[dest] + from_partner[dest]
+        return carry
+
+    lag_up = LAG * jnp.maximum(z - 1, 0)
+    lag_down = LAG * jnp.maximum(chips - 2 - z, 0)
+    from_below = (z > 0).astype(jnp.int32) * (SPREAD * (chips - 1 - z) + lag_up)
+    from_above = (z < chips - 1).astype(jnp.int32) * (SPREAD * z + lag_down)
     finish = jnp.maximum(from_below, from_above)
 
-    def chain_step(index, carry):
-        step = index // pieces
-        piece = index % pieces
-        for way in (0, 1):
-            dest = (chips - 1 - step) if way == 0 else step
-            if way == 0:
-                here = jnp.logical_and(z > 0, dest >= z)
-            else:
-                here = jnp.logical_and(z < chips - 1, dest <= z)
-
-            @pl.when(here)
-            def _():
-                chain_copy(way, dest, piece).wait_recv()
-                sums[dest, piece] = sums[dest, piece] + arrived[way, dest, piece]
-
-                @pl.when(dest != z)
+    def slot_step(slot, carry):
+        first = sum((slot > at).astype(jnp.int32) for at in ready)
+        after = sum((slot >= at).astype(jnp.int32) for at in ready)
+        lax.fori_loop(first, after, slab_step, 0)
+
+        def rank_step(rank, inner):
+            for way in (0, 1):
+                if way == 0:
+                    dest = chips - 1 - rank
+                    piece = slot - SPREAD * rank - lag_up
+                    waits = jnp.logical_and(z > 0, dest >= z)
+                    sends = dest > z
+                else:
+                    dest = rank
+                    piece = slot - SPREAD * rank - lag_down
+                    waits = jnp.logical_and(z < chips - 1, dest <= z)
+                    sends = dest < z
+                live = jnp.logical_and(piece >= 0, piece < pieces)
+
+                @pl.when(jnp.logical_and(live, waits))
+                def _():
+                    chain_copy(way, dest, piece).wait_recv()
+                    sums[dest, piece] = sums[dest, piece] + arrived[way, dest, piece]
+
+                @pl.when(jnp.logical_and(live, sends))
                 def _():
                     chain_copy(way, dest, piece).start()
 
-        @pl.when(step == finish)
+            return inner
+
+        lax.fori_loop(0, chips, rank_step, 0)
+
+        done = slot - finish
+
+        @pl.when(jnp.logical_and(done >= 0, done < pieces))
         def _():
             for offset in range(1, times):
-                peer_copy(offset, piece).start()
-
-        return carry
-
-    lax.fori_loop(0, chips * pieces, chain_step, 0)
+                peer_copy(offset, done).start()
+
+        @pl.when(slot == ready[-1] + 1)
+        def _():
+            split_factor()
+
+        return carry
+
+    lax.fori_loop(0, pieces + (SPREAD + LAG) * (chips - 1), slot_step, 0)
 
     def mix_step(piece, carry):
         mixed = sums[z, piece] * weights_ref[me, me]

time: 147 us -> 67.3 us (0.46)
  Pallas kernels: 143 us -> 62.4 us
    pallas_call x1, Pallas kernels: 143 us -> 62.4 us  [kernel_form(): pl.pallas_call(functools.partial(kernel, times, chips, normalizer), out_s...]
where the time goes in v2:
time: 67.3 us; the launch traced here: 66.3 us
  Pallas kernels  62.4 us (93%)
  local copies, waits for them, and re-layouts  3.23 us (5%)
    pallas_call x1, Pallas kernels, kernel_form(): pl.pallas_call(functools.partial(kernel, times, chips, normalizer), out_s...  62.4 us
    unnamed x2, local copies, waits for them, and re-layouts  3.23 us

profile of v2, /device:TPU:8, one launch (start us, length us, event | category | flops | bytes accessed | tf_op | source)
XLA Modules:
  0.0 66.3 jit_solution(17749430832536570550)
XLA Ops:
  0.7 1.3 %copy.9.factor_rows_ref = s32[8,3]{1,0:T(8,128)} copy(s32[8,3]{0,1:T(4,128)} %param.14) | data formatting | bytes 192 | tf_op args[6]
  2.0 62.4 %shard_map.82 = f32[1,128,1024]{2,1,0:T(8,128)} custom-call(s32[24]{0:T(128)} %pair_list_ref.1, s32[1]{0:T(128)S(6)} %copy.11.counts_ref, f32[4,4]{1,0:T(4,128)} %weights_ref.1, s32[8,3]{1,0:T(8,128)} %copy.9.factor_rows_ref, bf16[24,64,1024]{2,1,0:T(8,128)(2,1)} %three_ref.1, bf16[1,64,64,64]{3,2,1,0:T(8,128)(2,1)} %occ_ref.1, ...), custom_call_target="tpu_custom_call" | custom-call | tf_op jit(solution)/shard_map/pallas_call | solution.py:334
  64.4 1.9 %copy.12 = f32[1,128,1024]{2,1,0:T(8,128)} copy(f32[1,128,1024]{2,1,0:T(8,128)} %shard_map.82) | data formatting | bytes 1048576

commit v3 on v2

--- a/solution.py
+++ b/solution.py
@@ -10,7 +10,7 @@
 
 MESH = pl.DeviceIdType.MESH
 SPREAD = 3
-LAG = 2
+LAG = 3
 
 
 def slab_order(chips):

time: 67.3 us -> 64.6 us (0.960)
  Pallas kernels: 62.4 us -> 59.5 us
    pallas_call x1, Pallas kernels: 62.4 us -> 59.5 us  [kernel_form(): pl.pallas_call(functools.partial(kernel, times, chips, normalizer), out_s...]
where the time goes in v3:
time: 64.6 us; the launch traced here: 63.4 us
  Pallas kernels  59.5 us (92%)
  local copies, waits for them, and re-layouts  3.23 us (5%)
  between operations  0.66 us (1%)
    pallas_call x1, Pallas kernels, kernel_form(): pl.pallas_call(functools.partial(kernel, times, chips, normalizer), out_s...  59.5 us
    unnamed x2, local copies, waits for them, and re-layouts  3.23 us

profile of v3, /device:TPU:8, one launch (start us, length us, event | category | flops | bytes accessed | tf_op | source)
XLA Modules:
  0.0 63.4 jit_solution(11002527902952767537)
XLA Ops:
  0.7 1.3 %copy.9.factor_rows_ref = s32[8,3]{1,0:T(8,128)} copy(s32[8,3]{0,1:T(4,128)} %param.14) | data formatting | bytes 192 | tf_op args[6]
  2.0 59.5 %shard_map.82 = f32[1,128,1024]{2,1,0:T(8,128)} custom-call(s32[24]{0:T(128)} %pair_list_ref.1, s32[1]{0:T(128)S(6)} %copy.11.counts_ref, f32[4,4]{1,0:T(4,128)} %weights_ref.1, s32[8,3]{1,0:T(8,128)} %copy.9.factor_rows_ref, bf16[24,64,1024]{2,1,0:T(8,128)(2,1)} %three_ref.1, bf16[1,64,64,64]{3,2,1,0:T(8,128)(2,1)} %occ_ref.1, ...), custom_call_target="tpu_custom_call" | custom-call | tf_op jit(solution)/shard_map/pallas_call | solution.py:334
  61.5 1.9 %copy.12 = f32[1,128,1024]{2,1,0:T(8,128)} copy(f32[1,128,1024]{2,1,0:T(8,128)} %shard_map.82) | data formatting | bytes 1048576

commit v4 on v3

--- a/solution.py
+++ b/solution.py
@@ -87,7 +87,7 @@
     three_ref,
     occ_ref,
     vir_ref,
-    coulomb_ref,
+    coulomb_hbm,
     out_ref,
     left,
     right,
@@ -105,6 +105,8 @@
     chain_recv,
     peer_send,
     peer_recv,
+    factor,
+    factor_sem,
 ):
     slots, width, panel = three_ref.shape
     pieces, piece_rows = sums.shape[1], sums.shape[2]
@@ -115,6 +117,9 @@
     core = place % 2
     partner = z * 2 + 1 - core
 
+    factor_copy = pltpu.make_async_copy(coulomb_hbm, factor, factor_sem)
+    factor_copy.start()
+
     barrier = pltpu.get_barrier_semaphore()
     pl.semaphore_signal(barrier, inc=1, device_id={"pair": partner}, device_id_type=MESH)
     for offset in range(1, times):
@@ -186,14 +191,14 @@
             device_id_type=MESH,
         )
 
-    blocks, per_block, cb = coulomb_ref.shape[0], coulomb_ref.shape[1], coulomb_ref.shape[2]
+    blocks, per_block, cb = factor.shape[0], factor.shape[1], factor.shape[2]
 
     def split_factor():
         for block in range(blocks):
-            factor = coulomb_ref[block].reshape(per_block * cb, cb)
-            high = factor.astype(jnp.bfloat16)
+            exact = factor[block].reshape(per_block * cb, cb)
+            high = exact.astype(jnp.bfloat16)
             coulomb_high[block] = high
-            coulomb_low[block] = (factor - high.astype(jnp.float32)).astype(jnp.bfloat16)
+            coulomb_low[block] = (exact - high.astype(jnp.float32)).astype(jnp.bfloat16)
 
     order, ready = slab_order(chips)
 
@@ -257,6 +262,7 @@
 
         @pl.when(slot == ready[-1] + 1)
         def _():
+            factor_copy.wait()
             split_factor()
 
         return carry
@@ -334,7 +340,7 @@
     return pl.pallas_call(
         functools.partial(kernel, times, chips, normalizer),
         out_shape=jax.ShapeDtypeStruct((1, rows, panel), jnp.float32),
-        in_specs=[smem] * 4 + [vmem] * 4,
+        in_specs=[smem] * 4 + [vmem] * 3 + [pl.BlockSpec(memory_space=pl.ANY)],
         out_specs=vmem,
         scratch_shapes=[
             pltpu.VMEM((slots * width, panel), jnp.bfloat16),
@@ -353,6 +359,8 @@
             pltpu.SemaphoreType.DMA((2, chips, pieces)),
             pltpu.SemaphoreType.DMA((times - 1, pieces)),
             pltpu.SemaphoreType.DMA((times - 1, pieces)),
+            pltpu.VMEM(coulomb_blocks.shape, jnp.float32),
+            pltpu.SemaphoreType.DMA,
         ],
         compiler_params=pltpu.CompilerParams(
             collective_id=0, has_side_effects=True, vmem_limit_bytes=60 * 1024 * 1024

time: 64.6 us -> 64.1 us (level)
  no operation moved by 1% of the time
where the time goes in v4:
time: 64.1 us; the launch traced here: 62.8 us
  Pallas kernels  59 us (92%)
  local copies, waits for them, and re-layouts  3.23 us (5%)
  between operations  0.66 us (1%)
    pallas_call x1, Pallas kernels, kernel_form(): pl.pallas_call(functools.partial(kernel, times, chips, normalizer), out_s...  59 us
    unnamed x2, local copies, waits for them, and re-layouts  3.23 us

profile of v4, /device:TPU:8, one launch (start us, length us, event | category | flops | bytes accessed | tf_op | source)
XLA Modules:
  0.0 62.8 jit_solution(8203764085633020063)
XLA Ops:
  0.7 1.3 %copy.9.factor_rows_ref = s32[8,3]{1,0:T(8,128)} copy(s32[8,3]{0,1:T(4,128)} %param.14) | data formatting | bytes 192 | tf_op args[6]
  2.0 59.0 %shard_map.82 = f32[1,128,1024]{2,1,0:T(8,128)} custom-call(s32[24]{0:T(128)} %pair_list_ref.1, s32[1]{0:T(128)S(6)} %copy.11.counts_ref, f32[4,4]{1,0:T(4,128)} %weights_ref.1, s32[8,3]{1,0:T(8,128)} %copy.9.factor_rows_ref, bf16[24,64,1024]{2,1,0:T(8,128)(2,1)} %three_ref.1, bf16[1,64,64,64]{3,2,1,0:T(8,128)(2,1)} %occ_ref.1, ...), custom_call_target="tpu_custom_call" | custom-call | tf_op jit(solution)/shard_map/pallas_call | solution.py:340
  61.0 1.9 %copy.12 = f32[1,128,1024]{2,1,0:T(8,128)} copy(f32[1,128,1024]{2,1,0:T(8,128)} %shard_map.82) | data formatting | bytes 1048576
